TPU v7x, 128 devices: a whole 4x4x4 slice. The times are simulated.
128 devices in a mesh: dp: 8 (over y, core), expert: 16 (over z, x).
Axes of the slice: x: 4, y: 4, z: 4, core: 2. Of those that a mesh axis runs over, the one named last changes fastest.
Arguments:
- tokens: bfloat16 [16384, 3584], P(('dp', 'expert')), may hold values from -24 to 24
- cotangent: bfloat16 [16384, 3584], P(('dp', 'expert')), may hold values from -1.5 to 1.5
- gates: bfloat16 [16384, 2], P(('dp', 'expert')), may hold values from 0.19921875 to 1
- expert_ids: int32 [16384, 2], P(('dp', 'expert')), may hold values from 0 to 15, all different within a row; in each aligned block of 128 rows (0 to 127, 128 to 255, ...) at most 24 rows name the same one
- gate_w: bfloat16 [16, 3584, 1024], P('expert'), may hold values from -0.09375 to 0.09375
- up_w: bfloat16 [16, 3584, 1024], P('expert'), may hold values from -0.09375 to 0.09375
- down_w: bfloat16 [16, 1024, 3584], P('expert'), may hold values from -0.1875 to 0.1875
Outputs:
- grad_tokens: bfloat16 [16384, 3584], P('dp', 'expert')
- grad_gate_w: bfloat16 [16, 3584, 1024], P('expert', 'dp')
- grad_up_w: bfloat16 [16, 3584, 1024], P('expert', 'dp')
- grad_gates: bfloat16 [16384, 2], P(('dp', 'expert'))
Inputs may be any that keep to these rules, and one draw needn't show every extreme that they name: `expert_ids`: each token names 2 different experts; among the 128 tokens of one device no expert is named more than 24 times, and in every draw some expert is named exactly 24 times by some device's tokens.
All inputs are finite; a program needn't handle non-finite values.
Results may differ from a plain program's by a relative error of at most 0.014.
Values may be sent and summed in bfloat16 or wider, within the bound.
A program may use at most 192 MiB of HBM per device.

v0:
```python
import functools
import jax
import jax.numpy as jnp
from jax import lax
from jax.experimental import pallas as pl
from jax.experimental.pallas import tpu as pltpu
from jax.sharding import PartitionSpec as P

MESH = pl.DeviceIdType.MESH
BF = jnp.bfloat16
F32 = jnp.float32
LANES = 128


def grid_of(count):
    side = 1
    while side * side * 4 <= count:
        side *= 2
    return count // side, side


def dot_nt(left, right):
    return lax.dot_general(left, right, (((1,), (1,)), ((), ())), preferred_element_type=F32)


def kernel(
    n_dp,
    n_ex,
    cap,
    ids_ref,
    gts_ref,
    x_ref,
    y_ref,
    wg_hbm,
    wu_hbm,
    wd_hbm,
    gt_ref,
    gg_hbm,
    gu_hbm,
    gs_ref,
    wg,
    wu,
    wd,
    tgt,
    sx,
    sy,
    rx,
    ry,
    xt,
    av,
    bv,
    d2,
    score,
    ssend,
    sret,
    rg,
    rr,
    gath,
    xtg,
    dg,
    wo,
    wsem,
    tsend,
    trecv,
    xsend,
    xrecv,
    ysend,
    yrecv,
    psend,
    precv,
    qsend,
    dsend,
    drecv,
    dloc,
    rsend,
    rrecv,
    csend,
    crecv,
    osend,
    orecv,
    oloc,
    lsem,
):
    n_z, n_x = grid_of(n_ex)
    n_y = n_dp // 2
    tok, width = x_ref.shape
    hid = wg.shape[1]
    rows = n_ex * cap
    feat = width // n_ex
    deep = width // n_y
    half = deep // 2
    tile = min(256, hid)
    n_t = hid // tile
    me_e = lax.axis_index("expert")
    me_d = lax.axis_index("dp")
    pos_z, pos_x = me_e // n_x, me_e % n_x
    pos_y, core = me_d // 2, me_d % 2
    other = me_d + 1 - 2 * core

    def at(o):
        return ((pos_z + o // n_x) % n_z) * n_x + (pos_x + o % n_x) % n_x

    def copy_to(src, dst, send, recv, dp_id, ex_id):
        return pltpu.make_async_remote_copy(
            src_ref=src,
            dst_ref=dst,
            send_sem=send,
            recv_sem=recv,
            device_id=(dp_id, ex_id),
            device_id_type=MESH,
        )

    def slab(o):
        return pl.ds(o * (cap // 8), cap // 8)

    sx2, rx2 = sx.reshape(rows, width), rx.reshape(rows, width)
    sy2, ry2 = sy.reshape(rows, width + LANES), ry.reshape(rows, width + LANES)
    ssend2, sret2 = ssend.reshape(rows, LANES), sret.reshape(rows, LANES)

    def tiles(i):
        return pl.ds(pl.multiple_of(i * tile, tile), tile)

    loads = [
        pltpu.make_async_copy(wg_hbm, wg, wsem.at[0]),
        pltpu.make_async_copy(wu_hbm, wu, wsem.at[1]),
        pltpu.make_async_copy(wd_hbm, wd, wsem.at[2]),
    ]
    for load in loads:
        load.start()

    barrier = pltpu.get_barrier_semaphore()

    @pl.loop(1, n_ex)
    def _(o):
        pl.semaphore_signal(barrier, inc=1, device_id=(me_d, at(o)), device_id_type=MESH)

    @pl.loop(1, n_dp)
    def _(o):
        pl.semaphore_signal(
            barrier, inc=1, device_id=((me_d + o) % n_dp, me_e), device_id_type=MESH
        )

    ids = ids_ref[...]
    expert_no = lax.broadcasted_iota(jnp.int32, (n_ex, tok), 0)
    named = [(expert_no == ids[k : k + 1, :]).astype(F32) for k in range(2)]
    before = (
        lax.broadcasted_iota(jnp.int32, (tok, tok), 0)
        < lax.broadcasted_iota(jnp.int32, (tok, tok), 1)
    ).astype(F32)
    count = jnp.dot(
        (named[0] + named[1]).astype(BF), before.astype(BF), preferred_element_type=F32
    )
    place = [
        jnp.sum(named[k] * count, axis=0, keepdims=True) + (ids[k : k + 1, :] * cap).astype(F32)
        for k in range(2)
    ]
    slot_no = lax.broadcasted_iota(jnp.int32, (rows, tok), 0).astype(F32)
    picks = [(slot_no == place[k]).astype(F32) for k in range(2)]
    pick = (picks[0] + picks[1]).astype(BF)
    weight = jnp.sum(picks[0] * gts_ref[0:1, :] + picks[1] * gts_ref[1:2, :], axis=1, keepdims=True)
    row_no = lax.broadcasted_iota(jnp.int32, (8, tok), 0)
    tgt[me_e] = jnp.where(row_no == 0, place[0], place[1])

    pl.semaphore_wait(barrier, n_ex - 1 + n_dp - 1)

    def send_x(o):
        e = at(o)
        return copy_to(sx.at[slab(e)], rx.at[slab(o)], xsend.at[o], xrecv.at[o], me_d, e)

    def send_y(o):
        e = at(o)
        return copy_to(sy.at[slab(e)], ry.at[slab(o)], ysend.at[o], yrecv.at[o], me_d, e)

    def send_t(o):
        return copy_to(tgt.at[me_e], tgt.at[me_e], tsend.at[o], trecv.at[o], me_d, at(o))

    block = min(512, width)
    for i in range(width // block):
        span = slice(i * block, (i + 1) * block)
        sx2[:, span] = jnp.dot(pick, x_ref[:, span], preferred_element_type=F32).astype(BF)

    @pl.loop(1, n_ex)
    def _(o):
        send_x(o).start()
        send_t(o).start()

    own_x = pltpu.make_async_copy(sx.at[slab(me_e)], rx.at[slab(0)], lsem.at[0])
    own_x.start()
    for i in range(width // block):
        span = slice(i * block, (i + 1) * block)
        sy2[:, span] = jnp.dot(pick, y_ref[:, span], preferred_element_type=F32).astype(BF)
    sy2[:, width:] = jnp.broadcast_to(weight, (rows, LANES)).astype(BF)
    own_y = pltpu.make_async_copy(sy.at[slab(me_e)], ry.at[slab(0)], lsem.at[1])
    own_y.start()

    @pl.loop(1, n_ex)
    def _(o):
        send_x(o).wait_send()
        send_y(o).start()

    own_x.wait()

    @pl.loop(1, n_ex)
    def _(o):
        send_x(o).wait_recv()

    def send_p(r):
        chip = (pos_y + r) % n_y
        return copy_to(
            xt.at[pl.ds(pl.multiple_of(chip * deep, deep), deep)],
            xtg.at[me_d],
            psend.at[r],
            precv.at[me_d],
            chip * 2 + core,
            me_e,
        )

    def turn(r):
        chip = (pos_y + r) % n_y

        @pl.loop(0, deep // LANES)
        def _(i):
            start = pl.multiple_of(chip * deep + i * LANES, LANES)
            xt[pl.ds(start, LANES), :] = rx2[:, pl.ds(start, LANES)].T

    for r in [n_y // 2] + [r for r in range(1, n_y) if r != n_y // 2]:
        turn(r)
        send_p(r).start()
    turn(0)
    home = pl.ds(pl.multiple_of(pos_y * deep, deep), deep)
    own_p = pltpu.make_async_copy(xt.at[home], xtg.at[me_d], lsem.at[2])
    own_p.start()
    give_own = copy_to(xt.at[home], xtg.at[me_d], qsend.at[0], precv.at[me_d], other, me_e)
    give_own.start()

    loads[0].wait()
    loads[1].wait()

    @pl.loop(0, n_t)
    def _(i):
        av[:, tiles(i)] = jnp.dot(rx2[...], wg[:, tiles(i)], preferred_element_type=F32)
        bv[:, tiles(i)] = jnp.dot(rx2[...], wu[:, tiles(i)], preferred_element_type=F32)

    def relay(r):
        g = ((pos_y + n_y - r) % n_y) * 2 + core
        return copy_to(xtg.at[g], xtg.at[g], qsend.at[r], precv.at[g], other, me_e)

    @pl.loop(1, n_y)
    def _(r):
        relay(r).wait_recv()
        relay(r).start()

    own_y.wait()

    @pl.loop(1, n_ex)
    def _(o):
        send_y(o).wait_recv()

    loads[2].wait()
    score[...] = jnp.zeros_like(score)
    mine = pl.ds(pl.multiple_of(me_d * rows, rows), rows)

    def send_d(r, which, i):
        side = core if which == 0 else 1 - core
        chip = (pos_y + r) % n_y
        return copy_to(
            d2.at[side, :, tiles(i)],
            dg.at[mine, tiles(i)],
            dsend.at[(r * 2 + which) * n_t + i],
            drecv.at[me_d * n_t + i],
            chip * 2 + side,
            me_e,
        )

    def keep_d(i):
        return pltpu.make_async_copy(d2.at[core, :, tiles(i)], dg.at[mine, tiles(i)], dloc.at[i])

    @pl.loop(0, n_t)
    def _(i):
        back = dot_nt(ry2[:, :width], wd[tiles(i), :])
        a = av[:, tiles(i)]
        b = bv[:, tiles(i)]
        w = jnp.tile(ry2[:, width:].astype(F32), (1, tile // LANES))
        sig = jax.nn.sigmoid(a)
        silu = a * sig
        hidden = (silu * b).astype(BF)
        part = back * hidden.astype(F32)
        total = part[:, :LANES]
        for k in range(1, tile // LANES):
            total = total + part[:, k * LANES : (k + 1) * LANES]
        score[...] += total
        grad = back * w
        d2[0, :, tiles(i)] = (grad * b * sig * (1.0 + a * (1.0 - sig))).astype(BF)
        d2[1, :, tiles(i)] = (grad * silu).astype(BF)
        for r in [n_y // 2] + [r for r in range(1, n_y) if r != n_y // 2]:
            send_d(r, 0, i).start()
            send_d(r, 1, i).start()
        send_d(0, 1, i).start()
        keep_d(i).start()

    ssend2[...] = jnp.broadcast_to(jnp.sum(score[...], axis=1, keepdims=True), (rows, LANES)).astype(BF)

    def send_c(o):
        e = ((pos_z + n_z - o // n_x) % n_z) * n_x + (pos_x + n_x - o % n_x) % n_x
        return copy_to(ssend.at[slab(o)], sret.at[slab(me_e)], csend.at[o], crecv.at[o], me_d, e)

    @pl.loop(1, n_ex)
    def _(o):
        send_c(o).start()

    own_c = pltpu.make_async_copy(ssend.at[slab(0)], sret.at[slab(me_e)], lsem.at[3])
    own_c.start()

    def send_r(o):
        return copy_to(rg.at[o], rr.at[me_e], rsend.at[o], rrecv.at[o], me_d, at(o))

    own_r = pltpu.make_async_copy(rg.at[0], rr.at[me_e], lsem.at[4])

    def block_grad(o):
        span = pl.ds(pl.multiple_of(at(o) * feat, feat), feat)
        rg[o] = (dot_nt(d2[0], wg[span, :]) + dot_nt(d2[1], wu[span, :])).astype(BF)

    @pl.loop(1, n_ex)
    def _(o):
        block_grad(o)
        send_r(o).start()

    block_grad(0)
    own_r.start()

    @pl.loop(1, n_ex)
    def _(o):
        send_t(o).wait_recv()

    own_r.wait()

    @pl.loop(1, n_ex)
    def _(o):
        send_r(o).wait_recv()

    lane_no = lax.broadcasted_iota(jnp.int32, (tok, rows), 1).astype(F32)
    for s in range(n_ex):
        sz, sx_ = s // n_x, s % n_x
        column = tgt[s].T
        hit = (lane_no == column[:, 0:1]) | (lane_no == column[:, 1:2])
        choose = hit.astype(F32).astype(BF)
        for e in range(n_ex):
            o = ((e // n_x - sz) % n_z) * n_x + (e % n_x - sx_) % n_x
            gath[e * cap : (e + 1) * cap, :] = rr[e, o * cap : (o + 1) * cap, :]
        gt_ref[s * tok : (s + 1) * tok, :] = jnp.dot(
            choose, gath[...], preferred_element_type=F32
        ).astype(BF)

    own_c.wait()

    @pl.loop(1, n_ex)
    def _(o):
        send_c(o).wait_recv()

    column = tgt[me_e].T
    back_scores = sret2[...]
    first = jnp.dot(
        (lane_no == column[:, 0:1]).astype(F32).astype(BF), back_scores, preferred_element_type=F32
    )
    second = jnp.dot(
        (lane_no == column[:, 1:2]).astype(F32).astype(BF), back_scores, preferred_element_type=F32
    )
    which = lax.broadcasted_iota(jnp.int32, (tok, LANES), 1)
    gs_ref[...] = jnp.where(which == 0, first, second).astype(BF)[:, :2]

    own_p.wait()

    @pl.loop(0, n_y)
    def _(r):
        g = ((pos_y + r) % n_y) * 2 + 1 - core
        copy_to(xtg.at[g], xtg.at[g], qsend.at[0], precv.at[g], other, me_e).wait_recv()

    def own_half(i, out):
        return pltpu.make_async_copy(wo.at[core, :, tiles(i)], out.at[:, tiles(i)], oloc.at[i])

    def other_half(i, out):
        return copy_to(
            wo.at[1 - core, :, tiles(i)],
            out.at[:, tiles(i)],
            osend.at[i],
            orecv.at[i],
            other,
            me_e,
        )

    @pl.loop(0, n_t)
    def _(i):
        keep_d(i).wait()

        @pl.loop(1, n_dp)
        def _(r):
            g = (me_d + r) % n_dp
            there = pl.ds(pl.multiple_of(g * rows, rows), rows)
            copy_to(
                dg.at[there, tiles(i)],
                dg.at[there, tiles(i)],
                dsend.at[0],
                drecv.at[g * n_t + i],
                other,
                me_e,
            ).wait_recv()

        for h in range(2):
            acc = jnp.zeros((half, tile), F32)
            for g in range(n_dp):
                acc = acc + jnp.dot(
                    xtg[g, h * half : (h + 1) * half, :],
                    dg[g * rows : (g + 1) * rows, tiles(i)],
                    preferred_element_type=F32,
                )
            wo[h, :, tiles(i)] = (acc * (1.0 / n_dp)).astype(BF)

        @pl.when(core == 0)
        def _():
            own_half(i, gg_hbm).start()
            other_half(i, gg_hbm).start()

        @pl.when(core == 1)
        def _():
            own_half(i, gu_hbm).start()
            other_half(i, gu_hbm).start()

    @pl.loop(0, n_t)
    def _(i):
        own_half(i, gg_hbm).wait()
        other_half(i, gg_hbm).wait()

    @pl.loop(1, n_ex)
    def _(o):
        send_t(o).wait_send()
        send_y(o).wait_send()
        send_c(o).wait_send()
        send_r(o).wait_send()

    give_own.wait_send()

    @pl.loop(1, n_y)
    def _(r):
        send_p(r).wait_send()
        relay(r).wait_send()

    @pl.loop(0, n_t)
    def _(i):
        send_d(0, 1, i).wait_send()

        @pl.loop(1, n_y)
        def _(r):
            send_d(r, 0, i).wait_send()
            send_d(r, 1, i).wait_send()


def local(tokens, cotangent, gates, expert_ids, gate_w, up_w, down_w):
    tok, width = tokens.shape
    top = expert_ids.shape[1]
    n_ex = lax.axis_size("expert")
    n_dp = lax.axis_size("dp")
    cap = 3 * tok * top // (2 * n_ex)
    hid = gate_w.shape[2]
    rows = n_ex * cap
    feat = width // n_ex
    n_y = n_dp // 2
    deep = width // n_y
    n_t = hid // min(256, hid)
    vmem = pl.BlockSpec(memory_space=pltpu.VMEM)
    hbm = pl.BlockSpec(memory_space=pl.ANY)
    dma = pltpu.SemaphoreType.DMA
    scratch = [
        pltpu.VMEM((width, hid), BF),
        pltpu.VMEM((width, hid), BF),
        pltpu.VMEM((hid, width), BF),
        pltpu.VMEM((n_ex, 8, tok), F32),
        pltpu.VMEM((rows // 8, 8, width), BF),
        pltpu.VMEM((rows // 8, 8, width + LANES), BF),
        pltpu.VMEM((rows // 8, 8, width), BF),
        pltpu.VMEM((rows // 8, 8, width + LANES), BF),
        pltpu.VMEM((width, rows), BF),
        pltpu.VMEM((rows, hid), F32),
        pltpu.VMEM((rows, hid), F32),
        pltpu.VMEM((2, rows, hid), BF),
        pltpu.VMEM((rows, LANES), F32),
        pltpu.VMEM((rows // 8, 8, LANES), BF),
        pltpu.VMEM((rows // 8, 8, LANES), BF),
        pltpu.VMEM((n_ex, rows, feat), BF),
        pltpu.VMEM((n_ex, rows, feat), BF),
        pltpu.VMEM((rows, feat), BF),
        pltpu.VMEM((n_dp, deep, rows), BF),
        pltpu.VMEM((n_dp * rows, hid), BF),
        pltpu.VMEM((2, deep // 2, hid), BF),
        dma((3,)),
        dma((n_ex,)),
        dma((n_ex,)),
        dma((n_ex,)),
        dma((n_ex,)),
        dma((n_ex,)),
        dma((n_ex,)),
        dma((n_y,)),
        dma((n_dp,)),
        dma((n_y,)),
        dma((2 * n_y * n_t,)),
        dma((n_dp * n_t,)),
        dma((n_t,)),
        dma((n_ex,)),
        dma((n_ex,)),
        dma((n_ex,)),
        dma((n_ex,)),
        dma((n_t,)),
        dma((n_t,)),
        dma((n_t,)),
        dma((5,)),
    ]
    return pl.pallas_call(
        functools.partial(kernel, n_dp, n_ex, cap),
        out_shape=(
            jax.ShapeDtypeStruct((n_ex * tok, feat), BF),
            jax.ShapeDtypeStruct((width // n_dp, hid), BF),
            jax.ShapeDtypeStruct((width // n_dp, hid), BF),
            jax.ShapeDtypeStruct((tok, top), BF),
        ),
        in_specs=[vmem, vmem, vmem, vmem, hbm, hbm, hbm],
        out_specs=(vmem, hbm, hbm, vmem),
        scratch_shapes=scratch,
        compiler_params=pltpu.CompilerParams(
            collective_id=0, has_side_effects=True, vmem_limit_bytes=64 * 1024 * 1024
        ),
    )(
        expert_ids.T,
        gates.astype(F32).T,
        tokens,
        cotangent,
        gate_w[0],
        up_w[0],
        down_w[0],
    )


def shard(tokens, cotangent, gates, expert_ids, gate_w, up_w, down_w):
    grad_tokens, grad_gate, grad_up, grad_gates = local(
        tokens, cotangent, gates, expert_ids, gate_w, up_w, down_w
    )
    return grad_tokens, grad_gate[None], grad_up[None], grad_gates


def solution(mesh):
    placed = (
        P(("dp", "expert"), None),
        P(("dp", "expert"), None),
        P(("dp", "expert"), None),
        P(("dp", "expert"), None),
        P("expert", None, None),
        P("expert", None, None),
        P("expert", None, None),
    )
    return jax.shard_map(
        shard,
        mesh=mesh,
        in_specs=placed,
        out_specs=(
            P("dp", "expert"),
            P("expert", "dp", None),
            P("expert", "dp", None),
            P(("dp", "expert"), None),
        ),
        check_vma=False,
    )
```

profile of v0, /device:TPU:41, one launch (start us, length us, event | category | flops | bytes accessed | tf_op | source)
XLA Modules:
  0.0 180.9 jit_solution(8025464917778996614)
XLA Ops:
  0.6 1.2 convert_bitcast_fusion.gts_ref
  1.9 171.1 %shard_map.102 = (bf16[2048,224]{1,0:T(8,128)(2,1)}, bf16[448,1024]{1,0:T(8,128)(2,1)}, bf16[448,1024]{1,0:T(8,128)(2,1)}, bf16[128,2]{1,0:T(8,128)(2,1)}) custom-call(s32[2,128]{1,0:T(2,128)} %bitcast.13, f32[2,128]{1,0:T(2,128)} %convert_bitcast_fusion.gts_ref, bf16[128,3584]{1,0:T(8,128)(2,1)} %x_ref.1, bf16[128,3584]{1,0:T(8,128)(2,1)} %y_ref.1, ...), custom_call_target="tpu_custom_call" | custom-call | tf_op jit(solution)/shard_map/pallas_call | solution.py:516
  173.0 2.2 %copy.11 = bf16[2048,224]{0,1:T(8,128)(2,1)} copy(bf16[2048,224]{1,0:T(8,128)(2,1)} %get-tuple-element.12) | data formatting | bytes 1835008
  175.2 1.3 copy.12
  176.5 2.2 %copy.15 = bf16[1,448,1024]{2,1,0:T(8,128)(2,1)} copy(bf16[1,448,1024]{2,1,0:T(8,128)(2,1)} %bitcast.12) | data formatting | bytes 1835008
  178.7 2.2 %copy.16 = bf16[1,448,1024]{2,1,0:T(8,128)(2,1)} copy(bf16[1,448,1024]{2,1,0:T(8,128)(2,1)} %bitcast.11) | data formatting | bytes 1835008
where the time goes:
time: 181 us
  Pallas kernels  171 us (94%)
  local copies, waits for them, and re-layouts  7.89 us (4%)
    pallas_call x1, Pallas kernels, local(): pl.pallas_call(functools.partial(kernel, n_dp, n_ex, cap), out_shape=(jax...  171 us
    unnamed x4, local copies, waits for them, and re-layouts  7.89 us

commit v1 on v0

v1 whole, which is shorter than its diff:
```python
import functools
import jax
import jax.numpy as jnp
from jax import lax
from jax.experimental import pallas as pl
from jax.experimental.pallas import tpu as pltpu
from jax.sharding import PartitionSpec as P

MESH = pl.DeviceIdType.MESH
BF = jnp.bfloat16
F32 = jnp.float32
LANES = 128


def grid_of(count):
    side = 1
    while side * side * 4 <= count:
        side *= 2
    return count // side, side


def dot_nt(left, right):
    return lax.dot_general(left, right, (((1,), (1,)), ((), ())), preferred_element_type=F32)


def kernel(
    n_dp,
    n_ex,
    cap,
    ids_ref,
    gts_ref,
    x_hbm,
    y_hbm,
    wg_hbm,
    wu_hbm,
    wd_hbm,
    gt_ref,
    gg_hbm,
    gu_hbm,
    gs_ref,
    wg,
    wu,
    wd,
    held,
    tgt,
    sx,
    sy,
    rx,
    ry,
    av,
    bv,
    d2,
    score,
    ssend,
    sret,
    rg,
    rr,
    xg,
    dg,
    xtt,
    acc,
    wo,
    wsem,
    tsend,
    trecv,
    xsend,
    xrecv,
    ysend,
    yrecv,
    psend,
    precv,
    qsend,
    dsend,
    drecv,
    fsend,
    dloc,
    rsend,
    rrecv,
    csend,
    crecv,
    osend,
    orecv,
    oloc,
    lsem,
):
    n_z, n_x = grid_of(n_ex)
    n_y = n_dp // 2
    tok, width = held.shape
    hid = wg.shape[1]
    rows = n_ex * cap
    part = rows // 2
    eights = cap // 8
    span8 = part // 8
    feat = width // n_ex
    deep = width // n_y
    half = deep // 2
    tile = hid // 2
    wide = min(256, hid)
    n_w = hid // wide
    me_e = lax.axis_index("expert")
    me_d = lax.axis_index("dp")
    pos_z, pos_x = me_e // n_x, me_e % n_x
    pos_y, core = me_d // 2, me_d % 2
    other = me_d + 1 - 2 * core
    near = sorted({1, n_y - 1})
    hops = [r for r in [n_y // 2] + near if r]
    hops = sorted(set(hops), key=hops.index)

    signs = [(a, b) for b in range(n_x) for a in range(n_z)]
    signs.sort(key=lambda t: (min(t[0], n_z - t[0]) + min(t[1], n_x - t[1]), t))
    order = [t for t in signs if t[0] % 2 == 0] + [t for t in signs if t[0] % 2 == 1]
    size = n_ex // 2

    def to(q):
        return ((pos_z + order[q][0]) % n_z) * n_x + (pos_x + order[q][1]) % n_x

    def source(q):
        return ((pos_z + n_z - order[q][0]) % n_z), (pos_x + n_x - order[q][1]) % n_x

    def copy_to(src, dst, send, recv, dp_id, ex_id):
        return pltpu.make_async_remote_copy(
            src_ref=src,
            dst_ref=dst,
            send_sem=send,
            recv_sem=recv,
            device_id=(dp_id, ex_id),
            device_id_type=MESH,
        )

    def slab(o):
        return pl.ds(o * eights, eights)

    def tiles(i):
        return slice(i * tile, (i + 1) * tile)

    sx2, rx2 = sx.reshape(rows, width), rx.reshape(rows, width)
    sy2, ry2 = sy.reshape(rows, width + LANES), ry.reshape(rows, width + LANES)
    ssend2, sret2 = ssend.reshape(rows, LANES), sret.reshape(rows, LANES)
    xg2 = xg.reshape(2 * n_dp * part, deep)
    rr2 = rr.reshape(n_ex, rows, feat)

    load_x = pltpu.make_async_copy(x_hbm, held, lsem.at[7])
    load_y = pltpu.make_async_copy(y_hbm, held, lsem.at[8])
    load_x.start()
    loads = [
        pltpu.make_async_copy(wg_hbm, wg, wsem.at[0]),
        pltpu.make_async_copy(wu_hbm, wu, wsem.at[1]),
        pltpu.make_async_copy(wd_hbm, wd, wsem.at[2]),
    ]
    for load in loads:
        load.start()

    barrier = pltpu.get_barrier_semaphore()

    @pl.loop(1, n_ex)
    def _(o):
        partner = ((pos_z + o // n_x) % n_z) * n_x + (pos_x + o % n_x) % n_x
        pl.semaphore_signal(barrier, inc=1, device_id=(me_d, partner), device_id_type=MESH)

    @pl.loop(1, n_dp)
    def _(o):
        pl.semaphore_signal(
            barrier, inc=1, device_id=((me_d + o) % n_dp, me_e), device_id_type=MESH
        )

    ids = ids_ref[...]
    expert_no = lax.broadcasted_iota(jnp.int32, (n_ex, tok), 0)
    named = [(expert_no == ids[k : k + 1, :]).astype(F32) for k in range(2)]
    before = (
        lax.broadcasted_iota(jnp.int32, (tok, tok), 0)
        < lax.broadcasted_iota(jnp.int32, (tok, tok), 1)
    ).astype(F32)
    count = jnp.dot(
        (named[0] + named[1]).astype(BF), before.astype(BF), preferred_element_type=F32
    )
    place = [
        jnp.sum(named[k] * count, axis=0, keepdims=True) + (ids[k : k + 1, :] * cap).astype(F32)
        for k in range(2)
    ]
    slot_no = lax.broadcasted_iota(jnp.int32, (rows, tok), 0).astype(F32)
    picks = [(slot_no == place[k]).astype(F32) for k in range(2)]
    pick = (picks[0] + picks[1]).astype(BF)
    gts = gts_ref[...].astype(F32)
    weight = jnp.sum(picks[0] * gts[0:1, :] + picks[1] * gts[1:2, :], axis=1, keepdims=True)
    row_no = lax.broadcasted_iota(jnp.int32, (8, tok), 0)
    tgt[me_e] = jnp.where(row_no == 0, place[0], place[1])

    def send_x(q):
        e = to(q)
        return copy_to(sx.at[slab(e)], rx.at[slab(q)], xsend.at[q], xrecv.at[q], me_d, e)

    def send_y(q):
        e = to(q)
        return copy_to(sy.at[slab(e)], ry.at[slab(q)], ysend.at[q], yrecv.at[q], me_d, e)

    def send_t(q):
        return copy_to(tgt.at[me_e], tgt.at[me_e], tsend.at[q], trecv.at[q], me_d, to(q))

    block = min(512, width)
    load_x.wait()
    for i in range(width // block):
        span = slice(i * block, (i + 1) * block)
        sx2[:, span] = jnp.dot(pick, held[:, span], preferred_element_type=F32).astype(BF)

    load_y.start()
    pl.semaphore_wait(barrier, n_ex - 1 + n_dp - 1)
    for q in range(1, size):
        send_x(q).start()
    own_x = pltpu.make_async_copy(sx.at[slab(me_e)], rx.at[slab(0)], lsem.at[0])
    own_x.start()
    load_y.wait()
    for i in range(width // block):
        span = slice(i * block, (i + 1) * block)
        sy2[:, span] = jnp.dot(pick, held[:, span], preferred_element_type=F32).astype(BF)
    sy2[:, width:] = jnp.broadcast_to(weight, (rows, LANES)).astype(BF)
    for q in range(1, size):
        send_y(q).start()
    own_y = pltpu.make_async_copy(sy.at[slab(me_e)], ry.at[slab(0)], lsem.at[1])
    own_y.start()
    for q in range(size, n_ex):
        send_x(q).start()
    for q in range(size, n_ex):
        send_y(q).start()
    for q in range(1, n_ex):
        send_t(q).start()

    def features(chip):
        return pl.ds(pl.multiple_of(chip * deep, LANES), deep)

    def group8(g):
        return pl.ds(g * span8, span8)

    def send_p(c, r):
        chip = (pos_y + r) % n_y
        return copy_to(
            rx.at[c * span8 : (c + 1) * span8, :, features(chip)],
            xg.at[c, group8(me_d)],
            psend.at[c * n_y + r],
            precv.at[c * n_dp + me_d],
            chip * 2 + core,
            me_e,
        )

    def keep_p(c):
        return pltpu.make_async_copy(
            rx.at[c * span8 : (c + 1) * span8, :, features(pos_y)],
            xg.at[c, group8(me_d)],
            lsem.at[2 + c],
        )

    def give_p(c):
        return copy_to(
            rx.at[c * span8 : (c + 1) * span8, :, features(pos_y)],
            xg.at[c, group8(me_d)],
            qsend.at[c * n_y],
            precv.at[c * n_dp + me_d],
            other,
            me_e,
        )

    def relay_p(c, r):
        g = ((pos_y + n_y - r) % n_y) * 2 + core
        return copy_to(
            xg.at[c, group8(g)],
            xg.at[c, group8(g)],
            qsend.at[c * n_y + r],
            precv.at[c * n_dp + g],
            other,
            me_e,
        )

    def group(g):
        return pl.ds(pl.multiple_of(g * part, 16), part)

    def send_d(c, i, r, which):
        side = core if which == 0 else 1 - core
        chip = (pos_y + r) % n_y
        return copy_to(
            d2.at[c, side, :, tiles(i)],
            dg.at[c, group(me_d), tiles(i)],
            dsend.at[((c * 2 + i) * n_y + r) * 2 + which],
            drecv.at[(c * 2 + i) * n_dp + me_d],
            chip * 2 + side,
            me_e,
        )

    def keep_d(c, i):
        return pltpu.make_async_copy(
            d2.at[c, core, :, tiles(i)], dg.at[c, group(me_d), tiles(i)], dloc.at[c * 2 + i]
        )

    def all_d(c, i):
        return [send_d(c, i, r, which) for r in near for which in (0, 1)] + [send_d(c, i, 0, 1)]

    def forward(c, i, side):
        origin = (pos_y + n_y - 1 + 2 * core) % n_y
        g = origin * 2 + side
        return copy_to(
            dg.at[c, group(g), tiles(i)],
            dg.at[c, group(g), tiles(i)],
            fsend.at[(c * 2 + i) * 2 + side],
            drecv.at[(c * 2 + i) * n_dp + g],
            ((pos_y + n_y + 1 - 2 * core) % n_y) * 2 + core,
            me_e,
        )

    def arrived_d(c, i, g):
        here = dg.at[c, group(g), tiles(i)]
        copy_to(here, here, fsend.at[0], drecv.at[(c * 2 + i) * n_dp + g], other, me_e).wait_recv()

    far = n_y > 2

    def pass_on(c):
        if far:
            for i in range(2):
                for side in range(2):
                    forward(c, i, side).wait_recv()
                    forward(c, i, side).start()

    def forward_stage(c):
        if c == 0:
            own_x.wait()
        for q in range(max(1, c * size), (c + 1) * size):
            send_x(q).wait_recv()
        for r in hops:
            send_p(c, r).start()
        keep_p(c).start()
        give_p(c).start()
        if c == 0:
            loads[0].wait()
            loads[1].wait()
        here = slice(c * part, (c + 1) * part)

        @pl.loop(0, n_w)
        def _(i):
            cols = pl.ds(pl.multiple_of(i * wide, wide), wide)
            av[:, cols] = jnp.dot(rx2[here, :], wg[:, cols], preferred_element_type=F32)
            bv[:, cols] = jnp.dot(rx2[here, :], wu[:, cols], preferred_element_type=F32)

    def hidden_stage(c):
        if c == 0:
            own_y.wait()
            loads[2].wait()
        for q in range(max(1, c * size), (c + 1) * size):
            send_y(q).wait_recv()
        here = slice(c * part, (c + 1) * part)
        score[...] = jnp.zeros_like(score)
        for i in range(2):

            @pl.loop(0, tile // wide)
            def _(k):
                cols = pl.ds(pl.multiple_of(i * tile + k * wide, wide), wide)
                back = dot_nt(ry2[here, :width], wd[cols, :])
                a = av[:, cols]
                b = bv[:, cols]
                w = jnp.tile(ry2[here, width:].astype(F32), (1, wide // LANES))
                sig = jax.nn.sigmoid(a)
                silu = a * sig
                hidden = (silu * b).astype(BF)
                piece = back * hidden.astype(F32)
                total = piece[:, :LANES]
                for n in range(1, wide // LANES):
                    total = total + piece[:, n * LANES : (n + 1) * LANES]
                score[...] += total
                grad = back * w
                d2[c, 0, :, cols] = (grad * b * sig * (1.0 + a * (1.0 - sig))).astype(BF)
                d2[c, 1, :, cols] = (grad * silu).astype(BF)

            for copy in all_d(c, i):
                copy.start()
            keep_d(c, i).start()
        ssend2[here, :] = jnp.broadcast_to(
            jnp.sum(score[...], axis=1, keepdims=True), (part, LANES)
        ).astype(BF)
        for q in range(max(1, c * size), (c + 1) * size):
            send_c(q).start()
        if c == 0:
            own_c.start()

    def send_c(q):
        z, x = source(q)
        return copy_to(
            ssend.at[slab(q)], sret.at[slab(me_e)], csend.at[q], crecv.at[q], me_d, z * n_x + x
        )

    own_c = pltpu.make_async_copy(ssend.at[slab(0)], sret.at[slab(me_e)], lsem.at[4])

    def landing(c):
        return rr.at[:, (pos_z + c) % 2, :, me_e]

    def send_r(c, q):
        return copy_to(
            rg.at[c, q],
            landing(c),
            rsend.at[c * n_ex + q],
            rrecv.at[c * n_ex + q],
            me_d,
            to(q),
        )

    def keep_r(c):
        return pltpu.make_async_copy(rg.at[c, 0], landing(c), lsem.at[5 + c])

    def row_stage(c):
        for q in list(range(1, n_ex)) + [0]:
            span = pl.ds(pl.multiple_of(to(q) * feat, 16), feat)
            grad = (dot_nt(d2[c, 0], wg[span, :]) + dot_nt(d2[c, 1], wu[span, :])).astype(BF)
            for n in range(size):
                z, x = source(c * size + n)
                rg[c, q, z // 2, x] = grad[n * cap : (n + 1) * cap, :].reshape(eights, 8, feat)
            if q:
                send_r(c, q).start()
            else:
                keep_r(c).start()

    def relay_stage(c):
        for r in hops:
            relay_p(c, r).wait_recv()
            relay_p(c, r).start()

    def transpose_stage(c):
        keep_p(c).wait()

        @pl.loop(0, n_y)
        def _(r):
            g = ((pos_y + r) % n_y) * 2 + 1 - core
            here = xg.at[c, group8(g)]
            copy_to(here, here, qsend.at[0], precv.at[c * n_dp + g], other, me_e).wait_recv()

        base = c * n_dp * part
        for m in range(deep // LANES):
            xtt[m * LANES : (m + 1) * LANES, :] = xg2[
                base : base + n_dp * part, m * LANES : (m + 1) * LANES
            ].T

    def gathered(c, i):
        keep_d(c, i).wait()
        arrived_d(c, i, other)
        for r in range(1, n_y):
            chip = (pos_y + r) % n_y

            for side in range(2):
                g = chip * 2 + side
                if far and r == 1:
                    @pl.when(core == 0)
                    def _():
                        arrived_d(c, i, g)

                elif far and r == n_y - 1:

                    @pl.when(core == 1)
                    def _():
                        arrived_d(c, i, g)

                else:
                    arrived_d(c, i, g)

    def own_half(i, out):
        cols = pl.ds(pl.multiple_of(i * wide, wide), wide)
        return pltpu.make_async_copy(wo.at[core, :, cols], out.at[:, cols], oloc.at[i])

    def other_half(i, out):
        cols = pl.ds(pl.multiple_of(i * wide, wide), wide)
        return copy_to(
            wo.at[1 - core, :, cols],
            out.at[:, cols],
            osend.at[i],
            orecv.at[i],
            other,
            me_e,
        )

    forward_stage(0)
    hidden_stage(0)
    relay_stage(0)
    row_stage(0)
    forward_stage(1)
    pass_on(0)
    hidden_stage(1)
    relay_stage(1)
    row_stage(1)

    transpose_stage(0)
    for i in range(2):
        gathered(0, i)

    @pl.loop(0, n_w)
    def _(i):
        cols = pl.ds(pl.multiple_of(i * wide, wide), wide)
        acc[:, cols] = jnp.dot(xtt[...], dg[0, :, cols], preferred_element_type=F32)

    pass_on(1)
    transpose_stage(1)

    for q in range(1, n_ex):
        send_t(q).wait_recv()
    for c in range(2):
        keep_r(c).wait()
        for q in range(1, n_ex):
            send_r(c, q).wait_recv()

    lane_no = lax.broadcasted_iota(jnp.int32, (tok, rows), 1).astype(F32)
    for s in range(n_ex):
        z, x = s // n_x, s % n_x
        column = tgt[s].T
        hit = (lane_no == column[:, 0:1]) | (lane_no == column[:, 1:2])
        choose = hit.astype(F32).astype(BF)
        place_no = ((z // 2) * 2 + z % 2) * n_x + x
        gt_ref[s * tok : (s + 1) * tok, :] = jnp.dot(
            choose, rr2[place_no], preferred_element_type=F32
        ).astype(BF)

    for i in range(2):
        gathered(1, i)

    @pl.loop(0, n_w)
    def _(i):
        cols = pl.ds(pl.multiple_of(i * wide, wide), wide)
        total = acc[:, cols] + jnp.dot(xtt[...], dg[1, :, cols], preferred_element_type=F32)
        total = (total * (1.0 / n_dp)).astype(BF)
        wo[0, :, cols] = total[:half]
        wo[1, :, cols] = total[half:]

        @pl.when(core == 0)
        def _():
            own_half(i, gg_hbm).start()
            other_half(i, gg_hbm).start()

        @pl.when(core == 1)
        def _():
            own_half(i, gu_hbm).start()
            other_half(i, gu_hbm).start()

    own_c.wait()
    for q in range(1, n_ex):
        send_c(q).wait_recv()
    column = tgt[me_e].T
    back_scores = sret2[...]
    first = jnp.dot(
        (lane_no == column[:, 0:1]).astype(F32).astype(BF), back_scores, preferred_element_type=F32
    )
    second = jnp.dot(
        (lane_no == column[:, 1:2]).astype(F32).astype(BF), back_scores, preferred_element_type=F32
    )
    which = lax.broadcasted_iota(jnp.int32, (tok, LANES), 1)
    gs_ref[...] = jnp.where(which == 0, first, second).astype(BF)[:, :2]

    for q in range(1, n_ex):
        send_t(q).wait_send()
        send_x(q).wait_send()
        send_y(q).wait_send()
        send_c(q).wait_send()
        for c in range(2):
            send_r(c, q).wait_send()
    for c in range(2):
        give_p(c).wait_send()
        for r in hops:
            send_p(c, r).wait_send()
            relay_p(c, r).wait_send()
        for i in range(2):
            for copy in all_d(c, i):
                copy.wait_send()
            if far:
                for side in range(2):
                    forward(c, i, side).wait_send()

    @pl.loop(0, n_w)
    def _(i):
        own_half(i, gg_hbm).wait()
        other_half(i, gg_hbm).wait()


def local(tokens, cotangent, gates, expert_ids, gate_w, up_w, down_w):
    tok, width = tokens.shape
    top = expert_ids.shape[1]
    n_ex = lax.axis_size("expert")
    n_dp = lax.axis_size("dp")
    cap = 3 * tok * top // (2 * n_ex)
    hid = gate_w.shape[2]
    rows = n_ex * cap
    feat = width // n_ex
    n_y = n_dp // 2
    deep = width // n_y
    n_w = hid // min(256, hid)
    vmem = pl.BlockSpec(memory_space=pltpu.VMEM)
    hbm = pl.BlockSpec(memory_space=pl.ANY)
    dma = pltpu.SemaphoreType.DMA
    part = rows // 2
    n_z, n_x = grid_of(n_ex)
    scratch = [
        pltpu.VMEM((width, hid), BF),
        pltpu.VMEM((width, hid), BF),
        pltpu.VMEM((hid, width), BF),
        pltpu.VMEM((tok, width), BF),
        pltpu.VMEM((n_ex, 8, tok), F32),
        pltpu.VMEM((rows // 8, 8, width), BF),
        pltpu.VMEM((rows // 8, 8, width + LANES), BF),
        pltpu.VMEM((rows // 8, 8, width), BF),
        pltpu.VMEM((rows // 8, 8, width + LANES), BF),
        pltpu.VMEM((part, hid), F32),
        pltpu.VMEM((part, hid), F32),
        pltpu.VMEM((2, 2, part, hid), BF),
        pltpu.VMEM((part, LANES), F32),
        pltpu.VMEM((rows // 8, 8, LANES), BF),
        pltpu.VMEM((rows // 8, 8, LANES), BF),
        pltpu.VMEM((2, n_ex, n_z // 2, n_x, cap // 8, 8, feat), BF),
        pltpu.VMEM((n_z // 2, 2, n_x, n_ex, cap // 8, 8, feat), BF),
        pltpu.VMEM((2, n_dp * part // 8, 8, deep), BF),
        pltpu.VMEM((2, n_dp * part, hid), BF),
        pltpu.VMEM((deep, n_dp * part), BF),
        pltpu.VMEM((deep, hid), F32),
        pltpu.VMEM((2, deep // 2, hid), BF),
        dma((3,)),
        dma((n_ex,)),
        dma((n_ex,)),
        dma((n_ex,)),
        dma((n_ex,)),
        dma((n_ex,)),
        dma((n_ex,)),
        dma((2 * n_y,)),
        dma((2 * n_dp,)),
        dma((2 * n_y,)),
        dma((8 * n_y,)),
        dma((4 * n_dp,)),
        dma((8,)),
        dma((4,)),
        dma((2 * n_ex,)),
        dma((2 * n_ex,)),
        dma((n_ex,)),
        dma((n_ex,)),
        dma((n_w,)),
        dma((n_w,)),
        dma((n_w,)),
        dma((9,)),
    ]
    return pl.pallas_call(
        functools.partial(kernel, n_dp, n_ex, cap),
        out_shape=(
            jax.ShapeDtypeStruct((n_ex * tok, feat), BF),
            jax.ShapeDtypeStruct((width // n_dp, hid), BF),
            jax.ShapeDtypeStruct((width // n_dp, hid), BF),
            jax.ShapeDtypeStruct((tok, top), BF),
        ),
        in_specs=[vmem, vmem, hbm, hbm, hbm, hbm, hbm],
        out_specs=(vmem, hbm, hbm, vmem),
        scratch_shapes=scratch,
        compiler_params=pltpu.CompilerParams(
            collective_id=0, has_side_effects=True, vmem_limit_bytes=64 * 1024 * 1024
        ),
    )(
        expert_ids.T,
        gates.T,
        tokens,
        cotangent,
        gate_w[0],
        up_w[0],
        down_w[0],
    )


def settle(*refs):
    count = (len(refs) - 1) // 2
    copies = [
        pltpu.make_async_copy(refs[k], refs[count + k], refs[-1].at[k]) for k in range(count)
    ]
    for copy in copies:
        copy.start()
    for copy in copies:
        copy.wait()


def shard(tokens, cotangent, gates, expert_ids, gate_w, up_w, down_w):
    results = local(tokens, cotangent, gates, expert_ids, gate_w, up_w, down_w)
    hbm = pl.BlockSpec(memory_space=pl.ANY)
    grad_tokens, grad_gate, grad_up, grad_gates = pl.pallas_call(
        settle,
        out_shape=tuple(jax.ShapeDtypeStruct(r.shape, r.dtype) for r in results),
        in_specs=[hbm] * 4,
        out_specs=(hbm,) * 4,
        scratch_shapes=[pltpu.SemaphoreType.DMA((4,))],
    )(*results)
    return grad_tokens, grad_gate[None], grad_up[None], grad_gates


def solution(mesh):
    placed = (
        P(("dp", "expert"), None),
        P(("dp", "expert"), None),
        P(("dp", "expert"), None),
        P(("dp", "expert"), None),
        P("expert", None, None),
        P("expert", None, None),
        P("expert", None, None),
    )
    return jax.shard_map(
        shard,
        mesh=mesh,
        in_specs=placed,
        out_specs=(
            P("dp", "expert"),
            P("expert", "dp", None),
            P("expert", "dp", None),
            P(("dp", "expert"), None),
        ),
        check_vma=False,
    )
```

time: 181 us -> 226 us (1.25)
  the two profiles are of different devices: /device:TPU:41 before, /device:TPU:3 now
where the time goes in v1:
time: 226 us; the launch traced here: 224 us
  Pallas kernels  219 us (97%)
  local copies, waits for them, and re-layouts  3.57 us (2%)
    pallas_call x1, Pallas kernels, local(): pl.pallas_call(functools.partial(kernel, n_dp, n_ex, cap), out_shape=(jax...  130 us
    pallas_call x1, Pallas kernels, shard(): pl.pallas_call(settle, out_shape=tuple((jax.ShapeDtypeStruct(r.shape, r.d...  89.5 us

profile of v1, /device:TPU:3, one launch (start us, length us, event | category | flops | bytes accessed | tf_op | source)
XLA Modules:
  0.0 223.6 jit_solution(245218867049078926)
XLA Ops:
  0.6 129.9 %shard_map.102 = (bf16[2048,224]{1,0:T(8,128)(2,1)}, bf16[448,1024]{1,0:T(8,128)(2,1)}, bf16[448,1024]{1,0:T(8,128)(2,1)}, bf16[128,2]{1,0:T(8,128)(2,1)}) custom-call(s32[2,128]{1,0:T(2,128)} %bitcast.10, bf16[2,128]{1,0:T(2,128)(2,1)} %bitcast.11, bf16[128,3584]{1,0:T(8,128)(2,1)} %x_hbm.1, bf16[128,3584]{1,0:T(8,128)(2,1)} %y_hbm.1, ...), custom_call_target="tpu_custom_call" | custom-call | tf_op jit(solution)/shard_map/pallas_call | solution.py:636
  130.5 89.5 %shard_map.103 = (bf16[2048,224]{1,0:T(8,128)(2,1)}, bf16[448,1024]{1,0:T(8,128)(2,1)}, bf16[448,1024]{1,0:T(8,128)(2,1)}, bf16[128,2]{1,0:T(8,128)(2,1)}) custom-call(bf16[2048,224]{1,0:T(8,128)(2,1)} %get-tuple-element.12.refs_0_, bf16[448,1024]{1,0:T(8,128)(2,1)} %get-tuple-element.13.refs_1_, bf16[448,1024]{1,0:T(8,128)(2,1)} %get-tuple-element.14.refs_2_, ...), custom_call_target="tpu_custom_call" | custom-call | tf_op jit(solution)/shard_map/pallas_call | solution.py:675
  220.0 2.2 copy.11
  222.2 1.3 copy.12

commit v2 on v1

--- a/solution.py
+++ b/solution.py
@@ -51,6 +51,7 @@
     bv,
     d2,
     score,
+    wrow,
     ssend,
     sret,
     rg,
@@ -134,7 +135,7 @@
         return slice(i * tile, (i + 1) * tile)
 
     sx2, rx2 = sx.reshape(rows, width), rx.reshape(rows, width)
-    sy2, ry2 = sy.reshape(rows, width + LANES), ry.reshape(rows, width + LANES)
+    sy2, ry2 = sy.reshape(rows, width), ry.reshape(rows, width)
     ssend2, sret2 = ssend.reshape(rows, LANES), sret.reshape(rows, LANES)
     xg2 = xg.reshape(2 * n_dp * part, deep)
     rr2 = rr.reshape(n_ex, rows, feat)
@@ -181,9 +182,9 @@
     picks = [(slot_no == place[k]).astype(F32) for k in range(2)]
     pick = (picks[0] + picks[1]).astype(BF)
     gts = gts_ref[...].astype(F32)
-    weight = jnp.sum(picks[0] * gts[0:1, :] + picks[1] * gts[1:2, :], axis=1, keepdims=True)
-    row_no = lax.broadcasted_iota(jnp.int32, (8, tok), 0)
-    tgt[me_e] = jnp.where(row_no == 0, place[0], place[1])
+    tgt[me_e, 0:2, :] = jnp.concatenate(place, axis=0)
+    tgt[me_e, 2:4, :] = gts
+    tgt[me_e, 4:8, :] = jnp.zeros((4, tok), F32)
 
     def send_x(q):
         e = to(q)
@@ -192,6 +193,14 @@
     def send_y(q):
         e = to(q)
         return copy_to(sy.at[slab(e)], ry.at[slab(q)], ysend.at[q], yrecv.at[q], me_d, e)
+
+    def leave(src, dst, send, recv, chosen):
+        for n in range(eights):
+            for q in chosen:
+                e = to(q)
+                copy_to(
+                    src.at[e * eights + n], dst.at[q * eights + n], send.at[q], recv.at[q], me_d, e
+                ).start()
 
     def send_t(q):
         return copy_to(tgt.at[me_e], tgt.at[me_e], tsend.at[q], trecv.at[q], me_d, to(q))
@@ -204,25 +213,20 @@
 
     load_y.start()
     pl.semaphore_wait(barrier, n_ex - 1 + n_dp - 1)
-    for q in range(1, size):
-        send_x(q).start()
+    for q in range(1, n_ex):
+        send_t(q).start()
+    leave(sx, rx, xsend, xrecv, range(1, size))
     own_x = pltpu.make_async_copy(sx.at[slab(me_e)], rx.at[slab(0)], lsem.at[0])
     own_x.start()
     load_y.wait()
     for i in range(width // block):
         span = slice(i * block, (i + 1) * block)
         sy2[:, span] = jnp.dot(pick, held[:, span], preferred_element_type=F32).astype(BF)
-    sy2[:, width:] = jnp.broadcast_to(weight, (rows, LANES)).astype(BF)
-    for q in range(1, size):
-        send_y(q).start()
+    leave(sy, ry, ysend, yrecv, range(1, size))
     own_y = pltpu.make_async_copy(sy.at[slab(me_e)], ry.at[slab(0)], lsem.at[1])
     own_y.start()
-    for q in range(size, n_ex):
-        send_x(q).start()
-    for q in range(size, n_ex):
-        send_y(q).start()
-    for q in range(1, n_ex):
-        send_t(q).start()
+    leave(sx, rx, xsend, xrecv, range(size, n_ex))
+    leave(sy, ry, ysend, yrecv, range(size, n_ex))
 
     def features(chip):
         return pl.ds(pl.multiple_of(chip * deep, LANES), deep)
@@ -344,16 +348,28 @@
         for q in range(max(1, c * size), (c + 1) * size):
             send_y(q).wait_recv()
         here = slice(c * part, (c + 1) * part)
+        if c == 0:
+            for q in range(1, n_ex):
+                send_t(q).wait_recv()
+            slot_here = lax.broadcasted_iota(jnp.int32, (cap, tok), 0).astype(F32)
+            slot_here = slot_here + (me_e * cap).astype(F32)
+            for q in range(n_ex):
+                z, x = source(q)
+                note = tgt[z * n_x + x]
+                fit = jnp.where(slot_here == note[0:1, :], note[2:3, :], 0.0)
+                fit = fit + jnp.where(slot_here == note[1:2, :], note[3:4, :], 0.0)
+                fit = jnp.sum(fit, axis=1, keepdims=True)
+                wrow[q * cap : (q + 1) * cap, :] = jnp.broadcast_to(fit, (cap, LANES))
         score[...] = jnp.zeros_like(score)
         for i in range(2):
 
             @pl.loop(0, tile // wide)
             def _(k):
                 cols = pl.ds(pl.multiple_of(i * tile + k * wide, wide), wide)
-                back = dot_nt(ry2[here, :width], wd[cols, :])
+                back = dot_nt(ry2[here, :], wd[cols, :])
                 a = av[:, cols]
                 b = bv[:, cols]
-                w = jnp.tile(ry2[here, width:].astype(F32), (1, wide // LANES))
+                w = jnp.tile(wrow[here, :], (1, wide // LANES))
                 sig = jax.nn.sigmoid(a)
                 silu = a * sig
                 hidden = (silu * b).astype(BF)
@@ -492,22 +508,18 @@
     pass_on(1)
     transpose_stage(1)
 
-    for q in range(1, n_ex):
-        send_t(q).wait_recv()
     for c in range(2):
         keep_r(c).wait()
         for q in range(1, n_ex):
             send_r(c, q).wait_recv()
 
-    lane_no = lax.broadcasted_iota(jnp.int32, (tok, rows), 1).astype(F32)
     for s in range(n_ex):
         z, x = s // n_x, s % n_x
-        column = tgt[s].T
-        hit = (lane_no == column[:, 0:1]) | (lane_no == column[:, 1:2])
-        choose = hit.astype(F32).astype(BF)
+        note = tgt[s]
+        choose = ((slot_no == note[0:1, :]) | (slot_no == note[1:2, :])).astype(F32).astype(BF)
         place_no = ((z // 2) * 2 + z % 2) * n_x + x
-        gt_ref[s * tok : (s + 1) * tok, :] = jnp.dot(
-            choose, rr2[place_no], preferred_element_type=F32
+        gt_ref[:, s * tok : (s + 1) * tok] = lax.dot_general(
+            rr2[place_no], choose, (((0,), (0,)), ((), ())), preferred_element_type=F32
         ).astype(BF)
 
     for i in range(2):
@@ -534,16 +546,11 @@
     own_c.wait()
     for q in range(1, n_ex):
         send_c(q).wait_recv()
-    column = tgt[me_e].T
-    back_scores = sret2[...]
-    first = jnp.dot(
-        (lane_no == column[:, 0:1]).astype(F32).astype(BF), back_scores, preferred_element_type=F32
-    )
-    second = jnp.dot(
-        (lane_no == column[:, 1:2]).astype(F32).astype(BF), back_scores, preferred_element_type=F32
-    )
-    which = lax.broadcasted_iota(jnp.int32, (tok, LANES), 1)
-    gs_ref[...] = jnp.where(which == 0, first, second).astype(BF)[:, :2]
+    back_scores = sret2[...].astype(F32)
+    note = tgt[me_e]
+    for k in range(2):
+        found = jnp.where(slot_no == note[k : k + 1, :], back_scores, 0.0)
+        gs_ref[k : k + 1, :] = jnp.sum(found, axis=0, keepdims=True).astype(BF)
 
     for q in range(1, n_ex):
         send_t(q).wait_send()
@@ -594,13 +601,14 @@
         pltpu.VMEM((tok, width), BF),
         pltpu.VMEM((n_ex, 8, tok), F32),
         pltpu.VMEM((rows // 8, 8, width), BF),
-        pltpu.VMEM((rows // 8, 8, width + LANES), BF),
         pltpu.VMEM((rows // 8, 8, width), BF),
-        pltpu.VMEM((rows // 8, 8, width + LANES), BF),
+        pltpu.VMEM((rows // 8, 8, width), BF),
+        pltpu.VMEM((rows // 8, 8, width), BF),
         pltpu.VMEM((part, hid), F32),
         pltpu.VMEM((part, hid), F32),
         pltpu.VMEM((2, 2, part, hid), BF),
         pltpu.VMEM((part, LANES), F32),
+        pltpu.VMEM((rows, LANES), F32),
         pltpu.VMEM((rows // 8, 8, LANES), BF),
         pltpu.VMEM((rows // 8, 8, LANES), BF),
         pltpu.VMEM((2, n_ex, n_z // 2, n_x, cap // 8, 8, feat), BF),
@@ -636,10 +644,10 @@
     return pl.pallas_call(
         functools.partial(kernel, n_dp, n_ex, cap),
         out_shape=(
-            jax.ShapeDtypeStruct((n_ex * tok, feat), BF),
+            jax.ShapeDtypeStruct((feat, n_ex * tok), BF),
             jax.ShapeDtypeStruct((width // n_dp, hid), BF),
             jax.ShapeDtypeStruct((width // n_dp, hid), BF),
-            jax.ShapeDtypeStruct((tok, top), BF),
+            jax.ShapeDtypeStruct((top, tok), BF),
         ),
         in_specs=[vmem, vmem, hbm, hbm, hbm, hbm, hbm],
         out_specs=(vmem, hbm, hbm, vmem),
@@ -659,27 +667,23 @@
 
 
 def settle(*refs):
-    count = (len(refs) - 1) // 2
-    copies = [
-        pltpu.make_async_copy(refs[k], refs[count + k], refs[-1].at[k]) for k in range(count)
-    ]
-    for copy in copies:
-        copy.start()
-    for copy in copies:
-        copy.wait()
+    for k in range(4):
+        refs[4 + k][...] = refs[k][...]
 
 
 def shard(tokens, cotangent, gates, expert_ids, gate_w, up_w, down_w):
     results = local(tokens, cotangent, gates, expert_ids, gate_w, up_w, down_w)
-    hbm = pl.BlockSpec(memory_space=pl.ANY)
+    steps = 7
+    specs = [pl.BlockSpec((r.shape[0] // steps, r.shape[1]), lambda i: (i, 0)) for r in results[:3]]
+    specs.append(pl.BlockSpec(results[3].shape, lambda i: (0, 0)))
     grad_tokens, grad_gate, grad_up, grad_gates = pl.pallas_call(
         settle,
         out_shape=tuple(jax.ShapeDtypeStruct(r.shape, r.dtype) for r in results),
-        in_specs=[hbm] * 4,
-        out_specs=(hbm,) * 4,
-        scratch_shapes=[pltpu.SemaphoreType.DMA((4,))],
+        grid=(steps,),
+        in_specs=specs,
+        out_specs=tuple(specs),
     )(*results)
-    return grad_tokens, grad_gate[None], grad_up[None], grad_gates
+    return grad_tokens.T, grad_gate[None], grad_up[None], grad_gates.T
 
 
 def solution(mesh):

time: 226 us -> 131 us (0.58)
  Pallas kernels: 219 us -> 129 us
  local copies, waits for them, and re-layouts: 3.57 us -> 0 us
    pallas_call x1, Pallas kernels: 89.5 us -> 5.62 us  [shard(): pl.pallas_call(settle, out_shape=tuple((jax.ShapeDtypeStruct(r.shape, r.d...]
    pallas_call x1, Pallas kernels: 130 us -> 123 us  [local(): pl.pallas_call(functools.partial(kernel, n_dp, n_ex, cap), out_shape=(jax...]
    unnamed x2 -> x0, local copies, waits for them, and re-layouts: 3.57 us -> none
where the time goes in v2:
time: 131 us; the launch traced here: 129 us
  Pallas kernels  129 us (98%)
    pallas_call x1, Pallas kernels, local(): pl.pallas_call(functools.partial(kernel, n_dp, n_ex, cap), out_shape=(jax...  123 us
    pallas_call x1, Pallas kernels, shard(): pl.pallas_call(settle, out_shape=tuple((jax.ShapeDtypeStruct(r.shape, r.d...  5.62 us

profile of v2, /device:TPU:3, one launch (start us, length us, event | category | flops | bytes accessed | tf_op | source)
XLA Modules:
  0.0 129.4 jit_solution(2275305243701139324)
XLA Ops:
  0.6 123.1 %shard_map.102 = (bf16[224,2048]{1,0:T(8,128)(2,1)}, bf16[448,1024]{1,0:T(8,128)(2,1)}, bf16[448,1024]{1,0:T(8,128)(2,1)}, bf16[2,128]{1,0:T(2,128)(2,1)}) custom-call(s32[2,128]{1,0:T(2,128)} %bitcast.12, bf16[2,128]{1,0:T(2,128)(2,1)} %bitcast.13, bf16[128,3584]{1,0:T(8,128)(2,1)} %x_hbm.1, bf16[128,3584]{1,0:T(8,128)(2,1)} %y_hbm.1, ...), custom_call_target="tpu_custom_call" | custom-call | tf_op jit(solution)/shard_map/pallas_call | solution.py:644
  123.7 5.6 %shard_map.103 = (bf16[224,2048]{1,0:T(8,128)(2,1)}, bf16[448,1024]{1,0:T(8,128)(2,1)}, bf16[448,1024]{1,0:T(8,128)(2,1)}, bf16[2,128]{1,0:T(2,128)(2,1)}) custom-call(bf16[224,2048]{1,0:T(8,128)(2,1)} %get-tuple-element.12.refs_0_, bf16[448,1024]{1,0:T(8,128)(2,1)} %get-tuple-element.13.refs_1_, bf16[448,1024]{1,0:T(8,128)(2,1)} %get-tuple-element.14.refs_2_, ...), custom_call_target="tpu_custom_call" | custom-call | tf_op jit(solution)/shard_map/pallas_call | solution.py:679

commit v3 on v2

--- a/solution.py
+++ b/solution.py
@@ -10,6 +10,7 @@
 BF = jnp.bfloat16
 F32 = jnp.float32
 LANES = 128
+CHUNKS = 4
 
 
 def grid_of(count):
@@ -89,13 +90,12 @@
     tok, width = held.shape
     hid = wg.shape[1]
     rows = n_ex * cap
-    part = rows // 2
+    part = rows // CHUNKS
     eights = cap // 8
     span8 = part // 8
     feat = width // n_ex
     deep = width // n_y
     half = deep // 2
-    tile = hid // 2
     wide = min(256, hid)
     n_w = hid // wide
     me_e = lax.axis_index("expert")
@@ -109,8 +109,8 @@
 
     signs = [(a, b) for b in range(n_x) for a in range(n_z)]
     signs.sort(key=lambda t: (min(t[0], n_z - t[0]) + min(t[1], n_x - t[1]), t))
-    order = [t for t in signs if t[0] % 2 == 0] + [t for t in signs if t[0] % 2 == 1]
-    size = n_ex // 2
+    order = [t for n in range(CHUNKS) for t in signs if (t[0] % 2) * 2 + t[1] % 2 == n]
+    size = n_ex // CHUNKS
 
     def to(q):
         return ((pos_z + order[q][0]) % n_z) * n_x + (pos_x + order[q][1]) % n_x
@@ -131,17 +131,14 @@
     def slab(o):
         return pl.ds(o * eights, eights)
 
-    def tiles(i):
-        return slice(i * tile, (i + 1) * tile)
-
     sx2, rx2 = sx.reshape(rows, width), rx.reshape(rows, width)
     sy2, ry2 = sy.reshape(rows, width), ry.reshape(rows, width)
     ssend2, sret2 = ssend.reshape(rows, LANES), sret.reshape(rows, LANES)
-    xg2 = xg.reshape(2 * n_dp * part, deep)
+    xg2 = xg.reshape(CHUNKS * n_dp * part, deep)
     rr2 = rr.reshape(n_ex, rows, feat)
 
-    load_x = pltpu.make_async_copy(x_hbm, held, lsem.at[7])
-    load_y = pltpu.make_async_copy(y_hbm, held, lsem.at[8])
+    load_x = pltpu.make_async_copy(x_hbm, held, lsem.at[2])
+    load_y = pltpu.make_async_copy(y_hbm, held, lsem.at[3])
     load_x.start()
     loads = [
         pltpu.make_async_copy(wg_hbm, wg, wsem.at[0]),
@@ -225,8 +222,9 @@
     leave(sy, ry, ysend, yrecv, range(1, size))
     own_y = pltpu.make_async_copy(sy.at[slab(me_e)], ry.at[slab(0)], lsem.at[1])
     own_y.start()
-    leave(sx, rx, xsend, xrecv, range(size, n_ex))
-    leave(sy, ry, ysend, yrecv, range(size, n_ex))
+    for c in range(1, CHUNKS):
+        leave(sx, rx, xsend, xrecv, range(c * size, (c + 1) * size))
+        leave(sy, ry, ysend, yrecv, range(c * size, (c + 1) * size))
 
     def features(chip):
         return pl.ds(pl.multiple_of(chip * deep, LANES), deep)
@@ -249,7 +247,7 @@
         return pltpu.make_async_copy(
             rx.at[c * span8 : (c + 1) * span8, :, features(pos_y)],
             xg.at[c, group8(me_d)],
-            lsem.at[2 + c],
+            lsem.at[5 + c],
         )
 
     def give_p(c):
@@ -276,50 +274,47 @@
     def group(g):
         return pl.ds(pl.multiple_of(g * part, 16), part)
 
-    def send_d(c, i, r, which):
+    def send_d(c, r, which):
         side = core if which == 0 else 1 - core
         chip = (pos_y + r) % n_y
         return copy_to(
-            d2.at[c, side, :, tiles(i)],
-            dg.at[c, group(me_d), tiles(i)],
-            dsend.at[((c * 2 + i) * n_y + r) * 2 + which],
-            drecv.at[(c * 2 + i) * n_dp + me_d],
+            d2.at[c, side],
+            dg.at[c, group(me_d)],
+            dsend.at[(c * n_y + r) * 2 + which],
+            drecv.at[c * n_dp + me_d],
             chip * 2 + side,
             me_e,
         )
 
-    def keep_d(c, i):
-        return pltpu.make_async_copy(
-            d2.at[c, core, :, tiles(i)], dg.at[c, group(me_d), tiles(i)], dloc.at[c * 2 + i]
-        )
-
-    def all_d(c, i):
-        return [send_d(c, i, r, which) for r in near for which in (0, 1)] + [send_d(c, i, 0, 1)]
-
-    def forward(c, i, side):
+    def keep_d(c):
+        return pltpu.make_async_copy(d2.at[c, core], dg.at[c, group(me_d)], dloc.at[c])
+
+    def all_d(c):
+        return [send_d(c, r, which) for r in near for which in (0, 1)] + [send_d(c, 0, 1)]
+
+    def forward(c, side):
         origin = (pos_y + n_y - 1 + 2 * core) % n_y
         g = origin * 2 + side
         return copy_to(
-            dg.at[c, group(g), tiles(i)],
-            dg.at[c, group(g), tiles(i)],
-            fsend.at[(c * 2 + i) * 2 + side],
-            drecv.at[(c * 2 + i) * n_dp + g],
+            dg.at[c, group(g)],
+            dg.at[c, group(g)],
+            fsend.at[c * 2 + side],
+            drecv.at[c * n_dp + g],
             ((pos_y + n_y + 1 - 2 * core) % n_y) * 2 + core,
             me_e,
         )
 
-    def arrived_d(c, i, g):
-        here = dg.at[c, group(g), tiles(i)]
-        copy_to(here, here, fsend.at[0], drecv.at[(c * 2 + i) * n_dp + g], other, me_e).wait_recv()
+    def arrived_d(c, g):
+        here = dg.at[c, group(g)]
+        copy_to(here, here, fsend.at[0], drecv.at[c * n_dp + g], other, me_e).wait_recv()
 
     far = n_y > 2
 
     def pass_on(c):
         if far:
-            for i in range(2):
-                for side in range(2):
-                    forward(c, i, side).wait_recv()
-                    forward(c, i, side).start()
+            for side in range(2):
+                forward(c, side).wait_recv()
+                forward(c, side).start()
 
     def forward_stage(c):
         if c == 0:
@@ -361,30 +356,29 @@
                 fit = jnp.sum(fit, axis=1, keepdims=True)
                 wrow[q * cap : (q + 1) * cap, :] = jnp.broadcast_to(fit, (cap, LANES))
         score[...] = jnp.zeros_like(score)
-        for i in range(2):
-
-            @pl.loop(0, tile // wide)
-            def _(k):
-                cols = pl.ds(pl.multiple_of(i * tile + k * wide, wide), wide)
-                back = dot_nt(ry2[here, :], wd[cols, :])
-                a = av[:, cols]
-                b = bv[:, cols]
-                w = jnp.tile(wrow[here, :], (1, wide // LANES))
-                sig = jax.nn.sigmoid(a)
-                silu = a * sig
-                hidden = (silu * b).astype(BF)
-                piece = back * hidden.astype(F32)
-                total = piece[:, :LANES]
-                for n in range(1, wide // LANES):
-                    total = total + piece[:, n * LANES : (n + 1) * LANES]
-                score[...] += total
-                grad = back * w
-                d2[c, 0, :, cols] = (grad * b * sig * (1.0 + a * (1.0 - sig))).astype(BF)
-                d2[c, 1, :, cols] = (grad * silu).astype(BF)
-
-            for copy in all_d(c, i):
-                copy.start()
-            keep_d(c, i).start()
+
+        @pl.loop(0, n_w)
+        def _(k):
+            cols = pl.ds(pl.multiple_of(k * wide, wide), wide)
+            back = dot_nt(ry2[here, :], wd[cols, :])
+            a = av[:, cols]
+            b = bv[:, cols]
+            w = jnp.tile(wrow[here, :], (1, wide // LANES))
+            sig = jax.nn.sigmoid(a)
+            silu = a * sig
+            hidden = (silu * b).astype(BF)
+            piece = back * hidden.astype(F32)
+            total = piece[:, :LANES]
+            for n in range(1, wide // LANES):
+                total = total + piece[:, n * LANES : (n + 1) * LANES]
+            score[...] += total
+            grad = back * w
+            d2[c, 0, :, cols] = (grad * b * sig * (1.0 + a * (1.0 - sig))).astype(BF)
+            d2[c, 1, :, cols] = (grad * silu).astype(BF)
+
+        for copy in all_d(c):
+            copy.start()
+        keep_d(c).start()
         ssend2[here, :] = jnp.broadcast_to(
             jnp.sum(score[...], axis=1, keepdims=True), (part, LANES)
         ).astype(BF)
@@ -402,7 +396,7 @@
     own_c = pltpu.make_async_copy(ssend.at[slab(0)], sret.at[slab(me_e)], lsem.at[4])
 
     def landing(c):
-        return rr.at[:, (pos_z + c) % 2, :, me_e]
+        return rr.at[:, (pos_z + c // 2) % 2, :, (pos_x + c % 2) % 2, me_e]
 
     def send_r(c, q):
         return copy_to(
@@ -415,7 +409,7 @@
         )
 
     def keep_r(c):
-        return pltpu.make_async_copy(rg.at[c, 0], landing(c), lsem.at[5 + c])
+        return pltpu.make_async_copy(rg.at[c, 0], landing(c), lsem.at[9 + c])
 
     def row_stage(c):
         for q in list(range(1, n_ex)) + [0]:
@@ -423,7 +417,7 @@
             grad = (dot_nt(d2[c, 0], wg[span, :]) + dot_nt(d2[c, 1], wu[span, :])).astype(BF)
             for n in range(size):
                 z, x = source(c * size + n)
-                rg[c, q, z // 2, x] = grad[n * cap : (n + 1) * cap, :].reshape(eights, 8, feat)
+                rg[c, q, z // 2, x // 2] = grad[n * cap : (n + 1) * cap, :].reshape(eights, 8, feat)
             if q:
                 send_r(c, q).start()
             else:
@@ -449,27 +443,46 @@
                 base : base + n_dp * part, m * LANES : (m + 1) * LANES
             ].T
 
-    def gathered(c, i):
-        keep_d(c, i).wait()
-        arrived_d(c, i, other)
+    def gathered(c):
+        keep_d(c).wait()
+        arrived_d(c, other)
         for r in range(1, n_y):
-            chip = (pos_y + r) % n_y
-
             for side in range(2):
-                g = chip * 2 + side
-                if far and r == 1:
-                    @pl.when(core == 0)
+                g = ((pos_y + r) % n_y) * 2 + side
+                if far and r in near:
+                    @pl.when(core == (0 if r == 1 else 1))
                     def _():
-                        arrived_d(c, i, g)
-
-                elif far and r == n_y - 1:
-
-                    @pl.when(core == 1)
-                    def _():
-                        arrived_d(c, i, g)
+                        arrived_d(c, g)
 
                 else:
-                    arrived_d(c, i, g)
+                    arrived_d(c, g)
+
+    def weigh(c):
+        transpose_stage(c)
+        gathered(c)
+
+        @pl.loop(0, n_w)
+        def _(i):
+            cols = pl.ds(pl.multiple_of(i * wide, wide), wide)
+            total = jnp.dot(xtt[...], dg[c, :, cols], preferred_element_type=F32)
+            if c:
+                total = total + acc[:, cols]
+            if c < CHUNKS - 1:
+                acc[:, cols] = total
+            else:
+                total = (total * (1.0 / n_dp)).astype(BF)
+                wo[0, :, cols] = total[:half]
+                wo[1, :, cols] = total[half:]
+
+                @pl.when(core == 0)
+                def _():
+                    own_half(i, gg_hbm).start()
+                    other_half(i, gg_hbm).start()
+
+                @pl.when(core == 1)
+                def _():
+                    own_half(i, gu_hbm).start()
+                    other_half(i, gu_hbm).start()
 
     def own_half(i, out):
         cols = pl.ds(pl.multiple_of(i * wide, wide), wide)
@@ -486,62 +499,32 @@
             me_e,
         )
 
-    forward_stage(0)
-    hidden_stage(0)
-    relay_stage(0)
-    row_stage(0)
-    forward_stage(1)
-    pass_on(0)
-    hidden_stage(1)
-    relay_stage(1)
-    row_stage(1)
-
-    transpose_stage(0)
-    for i in range(2):
-        gathered(0, i)
-
-    @pl.loop(0, n_w)
-    def _(i):
-        cols = pl.ds(pl.multiple_of(i * wide, wide), wide)
-        acc[:, cols] = jnp.dot(xtt[...], dg[0, :, cols], preferred_element_type=F32)
-
-    pass_on(1)
-    transpose_stage(1)
-
-    for c in range(2):
+    for c in range(CHUNKS):
+        forward_stage(c)
+        hidden_stage(c)
+        if c:
+            pass_on(c - 1)
+        row_stage(c)
+        if c:
+            relay_stage(c - 1)
+        if c > 1:
+            weigh(c - 2)
+    weigh(CHUNKS - 2)
+    relay_stage(CHUNKS - 1)
+    pass_on(CHUNKS - 1)
+    weigh(CHUNKS - 1)
+
+    for c in range(CHUNKS):
         keep_r(c).wait()
         for q in range(1, n_ex):
             send_r(c, q).wait_recv()
 
     for s in range(n_ex):
-        z, x = s // n_x, s % n_x
         note = tgt[s]
         choose = ((slot_no == note[0:1, :]) | (slot_no == note[1:2, :])).astype(F32).astype(BF)
-        place_no = ((z // 2) * 2 + z % 2) * n_x + x
         gt_ref[:, s * tok : (s + 1) * tok] = lax.dot_general(
-            rr2[place_no], choose, (((0,), (0,)), ((), ())), preferred_element_type=F32
+            rr2[s], choose, (((0,), (0,)), ((), ())), preferred_element_type=F32
         ).astype(BF)
-
-    for i in range(2):
-        gathered(1, i)
-
-    @pl.loop(0, n_w)
-    def _(i):
-        cols = pl.ds(pl.multiple_of(i * wide, wide), wide)
-        total = acc[:, cols] + jnp.dot(xtt[...], dg[1, :, cols], preferred_element_type=F32)
-        total = (total * (1.0 / n_dp)).astype(BF)
-        wo[0, :, cols] = total[:half]
-        wo[1, :, cols] = total[half:]
-
-        @pl.when(core == 0)
-        def _():
-            own_half(i, gg_hbm).start()
-            other_half(i, gg_hbm).start()
-
-        @pl.when(core == 1)
-        def _():
-            own_half(i, gu_hbm).start()
-            other_half(i, gu_hbm).start()
 
     own_c.wait()
     for q in range(1, n_ex):
@@ -557,19 +540,18 @@
         send_x(q).wait_send()
         send_y(q).wait_send()
         send_c(q).wait_send()
-        for c in range(2):
+        for c in range(CHUNKS):
             send_r(c, q).wait_send()
-    for c in range(2):
+    for c in range(CHUNKS):
         give_p(c).wait_send()
         for r in hops:
             send_p(c, r).wait_send()
             relay_p(c, r).wait_send()
-        for i in range(2):
-            for copy in all_d(c, i):
-                copy.wait_send()
-            if far:
-                for side in range(2):
-                    forward(c, i, side).wait_send()
+        for copy in all_d(c):
+            copy.wait_send()
+        if far:
+            for side in range(2):
+                forward(c, side).wait_send()
 
     @pl.loop(0, n_w)
     def _(i):
@@ -592,7 +574,7 @@
     vmem = pl.BlockSpec(memory_space=pltpu.VMEM)
     hbm = pl.BlockSpec(memory_space=pl.ANY)
     dma = pltpu.SemaphoreType.DMA
-    part = rows // 2
+    part = rows // CHUNKS
     n_z, n_x = grid_of(n_ex)
     scratch = [
         pltpu.VMEM((width, hid), BF),
@@ -606,15 +588,15 @@
         pltpu.VMEM((rows // 8, 8, width), BF),
         pltpu.VMEM((part, hid), F32),
         pltpu.VMEM((part, hid), F32),
-        pltpu.VMEM((2, 2, part, hid), BF),
+        pltpu.VMEM((CHUNKS, 2, part, hid), BF),
         pltpu.VMEM((part, LANES), F32),
         pltpu.VMEM((rows, LANES), F32),
         pltpu.VMEM((rows // 8, 8, LANES), BF),
         pltpu.VMEM((rows // 8, 8, LANES), BF),
-        pltpu.VMEM((2, n_ex, n_z // 2, n_x, cap // 8, 8, feat), BF),
-        pltpu.VMEM((n_z // 2, 2, n_x, n_ex, cap // 8, 8, feat), BF),
-        pltpu.VMEM((2, n_dp * part // 8, 8, deep), BF),
-        pltpu.VMEM((2, n_dp * part, hid), BF),
+        pltpu.VMEM((CHUNKS, n_ex, n_z // 2, n_x // 2, cap // 8, 8, feat), BF),
+        pltpu.VMEM((n_z // 2, 2, n_x // 2, 2, n_ex, cap // 8, 8, feat), BF),
+        pltpu.VMEM((CHUNKS, n_dp * part // 8, 8, deep), BF),
+        pltpu.VMEM((CHUNKS, n_dp * part, hid), BF),
         pltpu.VMEM((deep, n_dp * part), BF),
         pltpu.VMEM((deep, hid), F32),
         pltpu.VMEM((2, deep // 2, hid), BF),
@@ -625,21 +607,21 @@
         dma((n_ex,)),
         dma((n_ex,)),
         dma((n_ex,)),
-        dma((2 * n_y,)),
-        dma((2 * n_dp,)),
-        dma((2 * n_y,)),
-        dma((8 * n_y,)),
-        dma((4 * n_dp,)),
-        dma((8,)),
-        dma((4,)),
-        dma((2 * n_ex,)),
-        dma((2 * n_ex,)),
+        dma((CHUNKS * n_y,)),
+        dma((CHUNKS * n_dp,)),
+        dma((CHUNKS * n_y,)),
+        dma((2 * CHUNKS * n_y,)),
+        dma((CHUNKS * n_dp,)),
+        dma((2 * CHUNKS,)),
+        dma((CHUNKS,)),
+        dma((CHUNKS * n_ex,)),
+        dma((CHUNKS * n_ex,)),
         dma((n_ex,)),
         dma((n_ex,)),
         dma((n_w,)),
         dma((n_w,)),
         dma((n_w,)),
-        dma((9,)),
+        dma((9 + CHUNKS,)),
     ]
     return pl.pallas_call(
         functools.partial(kernel, n_dp, n_ex, cap),
@@ -667,21 +649,40 @@
 
 
 def settle(*refs):
+    sources, results, held, sems = refs[:4], refs[4:8], refs[8:12], refs[12]
+    pieces = []
     for k in range(4):
-        refs[4 + k][...] = refs[k][...]
+        count = sources[k].shape[0]
+        cut = count // 2 if count % 32 == 0 else count
+        pieces += [(k, pl.ds(n, cut)) for n in range(0, count, cut)]
+    arrive = [
+        pltpu.make_async_copy(sources[k].at[span], held[k].at[span], sems.at[0, n])
+        for n, (k, span) in enumerate(pieces)
+    ]
+    depart = [
+        pltpu.make_async_copy(held[k].at[span], results[k].at[span], sems.at[1, n])
+        for n, (k, span) in enumerate(pieces)
+    ]
+    for copy in arrive:
+        copy.start()
+    for before, after in zip(arrive, depart):
+        before.wait()
+        after.start()
+    for copy in depart:
+        copy.wait()
 
 
 def shard(tokens, cotangent, gates, expert_ids, gate_w, up_w, down_w):
     results = local(tokens, cotangent, gates, expert_ids, gate_w, up_w, down_w)
-    steps = 7
-    specs = [pl.BlockSpec((r.shape[0] // steps, r.shape[1]), lambda i: (i, 0)) for r in results[:3]]
-    specs.append(pl.BlockSpec(results[3].shape, lambda i: (0, 0)))
+    hbm = pl.BlockSpec(memory_space=pl.ANY)
     grad_tokens, grad_gate, grad_up, grad_gates = pl.pallas_call(
         settle,
         out_shape=tuple(jax.ShapeDtypeStruct(r.shape, r.dtype) for r in results),
-        grid=(steps,),
-        in_specs=specs,
-        out_specs=tuple(specs),
+        in_specs=[hbm] * 4,
+        out_specs=(hbm,) * 4,
+        scratch_shapes=[pltpu.VMEM(r.shape, r.dtype) for r in results]
+        + [pltpu.SemaphoreType.DMA((2, 8))],
+        compiler_params=pltpu.CompilerParams(vmem_limit_bytes=16 * 1024 * 1024),
     )(*results)
     return grad_tokens.T, grad_gate[None], grad_up[None], grad_gates.T
 

time: 131 us -> 144 us (1.099)
  Pallas kernels: 129 us -> 139 us
  local copies, waits for them, and re-layouts: 0 us -> 4.1 us
    pallas_call x1, Pallas kernels: 123 us -> 135 us  [local(): pl.pallas_call(functools.partial(kernel, n_dp, n_ex, cap), out_shape=(jax...]
    unnamed x0 -> x8, local copies, waits for them, and re-layouts: none -> 4.1 us
    pallas_call x1, Pallas kernels: 5.62 us -> 3.28 us  [shard(): pl.pallas_call(settle, out_shape=tuple((jax.ShapeDtypeStruct(r.shape, r.d...]
where the time goes in v3:
time: 144 us
  Pallas kernels  139 us (97%)
  local copies, waits for them, and re-layouts  4.1 us (3%)
    pallas_call x1, Pallas kernels, local(): pl.pallas_call(functools.partial(kernel, n_dp, n_ex, cap), out_shape=(jax...  135 us
    unnamed x8, local copies, waits for them, and re-layouts  4.1 us
    pallas_call x1, Pallas kernels, shard(): pl.pallas_call(settle, out_shape=tuple((jax.ShapeDtypeStruct(r.shape, r.d...  3.28 us

profile of v3, /device:TPU:3, one launch (start us, length us, event | category | flops | bytes accessed | tf_op | source)
XLA Modules:
  0.0 143.7 jit_solution(8191440722413401355)
XLA Ops:
  0.6 135.5 %shard_map.102 = (bf16[224,2048]{1,0:T(8,128)(2,1)}, bf16[448,1024]{1,0:T(8,128)(2,1)}, bf16[448,1024]{1,0:T(8,128)(2,1)}, bf16[2,128]{1,0:T(2,128)(2,1)}) custom-call(s32[2,128]{1,0:T(2,128)} %bitcast.12, bf16[2,128]{1,0:T(2,128)(2,1)} %bitcast.13, bf16[128,3584]{1,0:T(8,128)(2,1)} %x_hbm.1, bf16[128,3584]{1,0:T(8,128)(2,1)} %y_hbm.1, ...), custom_call_target="tpu_custom_call" | custom-call | tf_op jit(solution)/shard_map/pallas_call | solution.py:626
  136.1 0.0 copy-start
  136.1 1.2 copy-done
  137.3 0.0 copy-start.1
  137.3 1.2 copy-done.1
  138.5 0.0 copy-start.2
  138.5 1.2 copy-done.2
  139.6 0.0 copy-start.3
  139.7 0.6 copy-done.3
  140.2 3.3 %shard_map.103 = (bf16[224,2048]{1,0:T(8,128)(2,1)}, bf16[448,1024]{1,0:T(8,128)(2,1)}, bf16[448,1024]{1,0:T(8,128)(2,1)}, bf16[2,128]{1,0:T(2,128)(2,1)}) custom-call(bf16[224,2048]{1,0:T(8,128)(2,1)S(1)} %copy-done, bf16[448,1024]{1,0:T(8,128)(2,1)S(1)} %copy-done.1, bf16[448,1024]{1,0:T(8,128)(2,1)S(1)} %copy-done.2, bf16[2,128]{1,0:T(2,128)(2,1)S(1)} %copy-done.3), custom_call_target="tpu_custom_call" | custom-call | tf_op jit(solution)/shard_map/pallas_call | solution.py:678
Async XLA Ops:
  136.1 1.2 copy-start
  137.3 1.2 copy-start.1
  138.5 1.2 copy-start.2
  139.6 0.6 copy-start.3

commit v4 on v2

--- a/solution.py
+++ b/solution.py
@@ -96,7 +96,7 @@
     deep = width // n_y
     half = deep // 2
     tile = hid // 2
-    wide = min(256, hid)
+    wide = min(256, tile)
     n_w = hid // wide
     me_e = lax.axis_index("expert")
     me_d = lax.axis_index("dp")
@@ -148,9 +148,6 @@
         pltpu.make_async_copy(wu_hbm, wu, wsem.at[1]),
         pltpu.make_async_copy(wd_hbm, wd, wsem.at[2]),
     ]
-    for load in loads:
-        load.start()
-
     barrier = pltpu.get_barrier_semaphore()
 
     @pl.loop(1, n_ex)
@@ -219,6 +216,8 @@
     own_x = pltpu.make_async_copy(sx.at[slab(me_e)], rx.at[slab(0)], lsem.at[0])
     own_x.start()
     load_y.wait()
+    for load in loads:
+        load.start()
     for i in range(width // block):
         span = slice(i * block, (i + 1) * block)
         sy2[:, span] = jnp.dot(pick, held[:, span], preferred_element_type=F32).astype(BF)
@@ -522,26 +521,26 @@
             rr2[place_no], choose, (((0,), (0,)), ((), ())), preferred_element_type=F32
         ).astype(BF)
 
-    for i in range(2):
-        gathered(1, i)
-
-    @pl.loop(0, n_w)
-    def _(i):
-        cols = pl.ds(pl.multiple_of(i * wide, wide), wide)
-        total = acc[:, cols] + jnp.dot(xtt[...], dg[1, :, cols], preferred_element_type=F32)
-        total = (total * (1.0 / n_dp)).astype(BF)
-        wo[0, :, cols] = total[:half]
-        wo[1, :, cols] = total[half:]
-
-        @pl.when(core == 0)
-        def _():
-            own_half(i, gg_hbm).start()
-            other_half(i, gg_hbm).start()
-
-        @pl.when(core == 1)
-        def _():
-            own_half(i, gu_hbm).start()
-            other_half(i, gu_hbm).start()
+    for k in range(2):
+        gathered(1, k)
+
+        @pl.loop(k * (n_w // 2), (k + 1) * (n_w // 2))
+        def _(i):
+            cols = pl.ds(pl.multiple_of(i * wide, wide), wide)
+            total = acc[:, cols] + jnp.dot(xtt[...], dg[1, :, cols], preferred_element_type=F32)
+            total = (total * (1.0 / n_dp)).astype(BF)
+            wo[0, :, cols] = total[:half]
+            wo[1, :, cols] = total[half:]
+
+            @pl.when(core == 0)
+            def _():
+                own_half(i, gg_hbm).start()
+                other_half(i, gg_hbm).start()
+
+            @pl.when(core == 1)
+            def _():
+                own_half(i, gu_hbm).start()
+                other_half(i, gu_hbm).start()
 
     own_c.wait()
     for q in range(1, n_ex):
@@ -588,7 +587,7 @@
     feat = width // n_ex
     n_y = n_dp // 2
     deep = width // n_y
-    n_w = hid // min(256, hid)
+    n_w = hid // min(256, hid // 2)
     vmem = pl.BlockSpec(memory_space=pltpu.VMEM)
     hbm = pl.BlockSpec(memory_space=pl.ANY)
     dma = pltpu.SemaphoreType.DMA
@@ -667,21 +666,40 @@
 
 
 def settle(*refs):
+    sources, results, held, sems = refs[:4], refs[4:8], refs[8:12], refs[12]
+    pieces = []
     for k in range(4):
-        refs[4 + k][...] = refs[k][...]
+        count = sources[k].shape[0]
+        cut = count // 2 if count % 32 == 0 else count
+        pieces += [(k, pl.ds(n, cut)) for n in range(0, count, cut)]
+    arrive = [
+        pltpu.make_async_copy(sources[k].at[span], held[k].at[span], sems.at[0, n])
+        for n, (k, span) in enumerate(pieces)
+    ]
+    depart = [
+        pltpu.make_async_copy(held[k].at[span], results[k].at[span], sems.at[1, n])
+        for n, (k, span) in enumerate(pieces)
+    ]
+    for copy in arrive:
+        copy.start()
+    for before, after in zip(arrive, depart):
+        before.wait()
+        after.start()
+    for copy in depart:
+        copy.wait()
 
 
 def shard(tokens, cotangent, gates, expert_ids, gate_w, up_w, down_w):
     results = local(tokens, cotangent, gates, expert_ids, gate_w, up_w, down_w)
-    steps = 7
-    specs = [pl.BlockSpec((r.shape[0] // steps, r.shape[1]), lambda i: (i, 0)) for r in results[:3]]
-    specs.append(pl.BlockSpec(results[3].shape, lambda i: (0, 0)))
+    hbm = pl.BlockSpec(memory_space=pltpu.HBM)
     grad_tokens, grad_gate, grad_up, grad_gates = pl.pallas_call(
         settle,
         out_shape=tuple(jax.ShapeDtypeStruct(r.shape, r.dtype) for r in results),
-        grid=(steps,),
-        in_specs=specs,
-        out_specs=tuple(specs),
+        in_specs=[hbm] * 4,
+        out_specs=(hbm,) * 4,
+        scratch_shapes=[pltpu.VMEM(r.shape, r.dtype) for r in results]
+        + [pltpu.SemaphoreType.DMA((2, 8))],
+        compiler_params=pltpu.CompilerParams(vmem_limit_bytes=16 * 1024 * 1024),
     )(*results)
     return grad_tokens.T, grad_gate[None], grad_up[None], grad_gates.T
 

time: 131 us -> 128 us (0.977)
  Pallas kernels: 129 us -> 121 us
  local copies, waits for them, and re-layouts: 0 us -> 4.1 us
    pallas_call x1, Pallas kernels: 123 us -> 118 us  [local(): pl.pallas_call(functools.partial(kernel, n_dp, n_ex, cap), out_shape=(jax...]
    unnamed x0 -> x8, local copies, waits for them, and re-layouts: none -> 4.1 us
    pallas_call x1, Pallas kernels: 5.62 us -> 3.28 us  [shard(): pl.pallas_call(settle, out_shape=tuple((jax.ShapeDtypeStruct(r.shape, r.d...]
where the time goes in v4:
time: 128 us; the launch traced here: 126 us
  Pallas kernels  121 us (95%)
  local copies, waits for them, and re-layouts  4.1 us (3%)
    pallas_call x1, Pallas kernels, local(): pl.pallas_call(functools.partial(kernel, n_dp, n_ex, cap), out_shape=(jax...  118 us
    unnamed x8, local copies, waits for them, and re-layouts  4.1 us
    pallas_call x1, Pallas kernels, shard(): pl.pallas_call(settle, out_shape=tuple((jax.ShapeDtypeStruct(r.shape, r.d...  3.28 us

profile of v4, /device:TPU:3, one launch (start us, length us, event | category | flops | bytes accessed | tf_op | source)
XLA Modules:
  0.0 126.1 jit_solution(8449901959295704669)
XLA Ops:
  0.6 117.9 %shard_map.102 = (bf16[224,2048]{1,0:T(8,128)(2,1)}, bf16[448,1024]{1,0:T(8,128)(2,1)}, bf16[448,1024]{1,0:T(8,128)(2,1)}, bf16[2,128]{1,0:T(2,128)(2,1)}) custom-call(s32[2,128]{1,0:T(2,128)} %bitcast.12, bf16[2,128]{1,0:T(2,128)(2,1)} %bitcast.13, bf16[128,3584]{1,0:T(8,128)(2,1)} %x_hbm.1, bf16[128,3584]{1,0:T(8,128)(2,1)} %y_hbm.1, ...), custom_call_target="tpu_custom_call" | custom-call | tf_op jit(solution)/shard_map/pallas_call | solution.py:643
  118.6 0.0 copy-start
  118.6 1.2 copy-done
  119.7 0.0 copy-start.1
  119.7 1.2 copy-done.1
  120.9 0.0 copy-start.2
  120.9 1.2 copy-done.2
  122.1 0.0 copy-start.3
  122.1 0.6 copy-done.3
  122.7 3.3 %shard_map.103 = (bf16[224,2048]{1,0:T(8,128)(2,1)}, bf16[448,1024]{1,0:T(8,128)(2,1)}, bf16[448,1024]{1,0:T(8,128)(2,1)}, bf16[2,128]{1,0:T(2,128)(2,1)}) custom-call(bf16[224,2048]{1,0:T(8,128)(2,1)S(1)} %copy-done, bf16[448,1024]{1,0:T(8,128)(2,1)S(1)} %copy-done.1, bf16[448,1024]{1,0:T(8,128)(2,1)S(1)} %copy-done.2, bf16[2,128]{1,0:T(2,128)(2,1)S(1)} %copy-done.3), custom_call_target="tpu_custom_call" | custom-call | tf_op jit(solution)/shard_map/pallas_call | solution.py:695
Async XLA Ops:
  118.6 1.2 copy-start
  119.7 1.2 copy-start.1
  120.9 1.2 copy-start.2
  122.1 0.6 copy-start.3
